TPU v7x, 256 devices: a whole 4x4x8 slice. The times are simulated.
256 devices in a mesh: group: 8 (over y, core), leaf: 32 (over z, x).
Axes of the slice: x: 4, y: 4, z: 8, core: 2. Of those that a mesh axis runs over, the one named last changes fastest.
Arguments:
- points: float32 [3, 524288], P(None, ('group', 'leaf')), may hold values from 0 to 1
- rhs: float32 [16, 524288], P(None, ('group', 'leaf')), may hold values from -0.5 to 0.5
- counts: int32 [4096], P(('group', 'leaf')), may hold values from 32 to 128
- basis: float32 [4096, 128, 32], P(('group', 'leaf')), may hold values from -1 to 1
- leaf_geom: float32 [4096, 4], P(('group', 'leaf')), may hold values from 0.05 to 1
- leaf_partners: int32 [4096, 16], P(('group', 'leaf')), may hold values from -16 to 16, as said below
- leaf_middle_owner: int32 [256, 16], P(('group', 'leaf')), may hold values from 0 to 7, never falling along the last dimension, each value on 1 to 4 neighbouring positions
- leaf_basis_transfer: float32 [4096, 32, 32], P(('group', 'leaf')), may hold values from -1 to 1
- mid_geom: float32 [2048, 4], P(('group', 'leaf')), may hold values from 0.05 to 1
- mid_parent: int32 [8, 256], P('group', 'leaf'), may hold values from 0 to 15, never falling along the last dimension, each value on 1 to 32 neighbouring positions
- mid_transfer: float32 [2048, 32, 32], P(('group', 'leaf')), may hold values from -1 to 1
- mid_peers: int32 [2048, 8], P(('group', 'leaf')), may hold values from 0 to 31, all different within a row; in each aligned block of 8 rows (0 to 7, 8 to 15, ...) at most 4 rows name the same one
- mid_slots: int32 [2048, 8], P(('group', 'leaf')), may hold values from 0 to 7
- top_geom: float32 [128, 4], P('group'), may hold values from 0.05 to 1
- top_offsets: int32 [128, 16], P('group'), may hold values from 1 to 127
Outputs:
- product: float32 [16, 524288], P(None, ('group', 'leaf'))
Inputs may be any that keep to these rules, and one draw needn't show every extreme that they name: `leaf_partners`: column 0 is 0. Every partner leaf lies in the same group, at most 16 leaves away. `mid_peers`: over the rows of one device, no device is named more than 4 times, and some device is named exactly 4 times; the names in a row differ. `leaf_middle_owner`: never falling along a row. `mid_parent`: never falling along a row.
All inputs are finite; a program needn't handle non-finite values.
Results may differ from a plain program's by a relative error of at most 0.00013.
Values sent between devices are 32-bit elements; how exact they have to be, the bound alone decides.
A program may use at most 64 MiB of HBM per device.

v0:
```python
import jax
import jax.numpy as jnp
from jax import lax
from jax.sharding import PartitionSpec as P

PTS = 128
RANK = 32
RHS = 16
TOP = 16
NEAR = 8
REACH = 16
exact_product = lax.Precision.HIGHEST
root_three = 1.7320508075688772
length_scale = 0.5


def extended(block, sides, width):
    for axis, dim in sides:
        count = lax.axis_size(axis)
        forward = [(i, i + 1) for i in range(count - 1)]
        backward = [(target, source) for source, target in forward]
        low = lax.ppermute(
            lax.slice_in_dim(block, block.shape[dim] - width, None, axis=dim), axis, forward
        )
        high = lax.ppermute(lax.slice_in_dim(block, 0, width, axis=dim), axis, backward)
        block = jnp.concatenate([low, block, high], axis=dim)
    return block


def node_table():
    indices = jnp.arange(RANK, dtype=jnp.int32)
    layers = []
    for axis_number in range(3):
        spread = (indices * (2 * axis_number + 3) % RANK).astype(jnp.float32)
        layers.append(jnp.cos(jnp.pi * (spread + 0.5) / RANK))
    return jnp.stack(layers)


def place_nodes(geometry, table):
    return geometry[..., :3, None] + geometry[..., 3:4, None] * table


def matern(left, right):
    squared = jnp.zeros((), jnp.float32)
    for axis_number in range(3):
        difference = left[..., axis_number, :, None] - right[..., axis_number, None, :]
        squared = squared + difference * difference
    distance = jnp.sqrt(squared)
    decay_rate = root_three / length_scale
    return (1.0 + decay_rate * distance) * jnp.exp(-decay_rate * distance)


def couple_rows(target_geom, source_point_rows, table):
    coeff_width = RANK * RHS
    target_nodes = place_nodes(target_geom, table)
    source_nodes = place_nodes(source_point_rows[..., coeff_width:], table)
    source_coeff = source_point_rows[..., :coeff_width].reshape(
        source_point_rows.shape[:-1] + (RANK, RHS)
    )
    coupling = matern(target_nodes[:, None], source_nodes)
    return jnp.einsum("njkm,njmr->nkr", coupling, source_coeff, precision=exact_product)


def on_device(
    points,
    rhs,
    counts,
    basis,
    leaf_geom,
    leaf_partners,
    leaf_middle_owner,
    leaf_basis_transfer,
    mid_geom,
    mid_parent,
    mid_transfer,
    mid_peers,
    mid_slots,
    top_geom,
    top_offsets,
):
    leaf_count = counts.shape[0]
    mid_count = mid_transfer.shape[0]
    coeff_width = RANK * RHS
    table = node_table()
    position = jnp.arange(PTS, dtype=jnp.int32)
    present = (position[None, :] < counts[:, None]).astype(jnp.float32)
    masked = rhs.reshape(RHS, leaf_count, PTS) * present[None]
    stacked = jnp.concatenate([masked.reshape(RHS, leaf_count * PTS), points], axis=0)
    padded = extended(stacked, (("leaf", 1),), REACH * PTS)
    grid = padded.reshape(RHS + 3, leaf_count + 2 * REACH, PTS)
    leaf_coefficient_rows = jnp.einsum("lpk,rlp->lkr", basis, masked, precision=exact_product)
    leaf_rows = jnp.concatenate(
        [leaf_coefficient_rows.reshape(leaf_count, coeff_width), leaf_geom], axis=1
    )
    leaf_padded = extended(leaf_rows, (("leaf", 0),), REACH)
    members = (
        leaf_middle_owner[0][None, :] == jnp.arange(mid_count, dtype=jnp.int32)[:, None]
    ).astype(jnp.float32)
    upward_coefficients = jnp.einsum(
        "qcz,qct->qzt", leaf_basis_transfer, leaf_coefficient_rows, precision=exact_product
    )
    coeff_mid = jnp.einsum("ml,ljr->mjr", members, upward_coefficients, precision=exact_product)
    mid_rows = jnp.concatenate([coeff_mid.reshape(mid_count, coeff_width), mid_geom], axis=1)
    top_members = (mid_parent[0][None, :] == jnp.arange(TOP, dtype=jnp.int32)[:, None]).astype(
        jnp.float32
    )
    raised = jnp.einsum("mkj,mkr->mjr", mid_transfer, coeff_mid, precision=exact_product)
    partial_top = jnp.einsum("tm,mjr->tjr", top_members, raised, precision=exact_product)
    coeff_top = lax.psum(partial_top, "leaf")
    top_rows = jnp.concatenate([coeff_top.reshape(TOP, coeff_width), top_geom], axis=1)
    top_all = lax.all_gather(top_rows, "group", axis=0, tiled=True)
    total_tops = top_all.shape[0]
    targets = lax.axis_index("group") * TOP + jnp.arange(TOP, dtype=jnp.int32)
    top_source = (targets[:, None] + top_offsets) % total_tops
    local_top = couple_rows(top_geom, top_all[top_source], table)
    mid_all = lax.all_gather(mid_rows, "leaf", axis=0, tiled=True)
    mid_source = mid_peers * mid_count + mid_slots
    source_point_rows = mid_all[mid_source]
    device_middle_index = jnp.einsum(
        "mkj,mjr->mkr", mid_transfer, local_top[mid_parent[0]], precision=exact_product
    )
    device_middle_index = device_middle_index + couple_rows(mid_geom, source_point_rows, table)
    leaf_index = jnp.arange(leaf_count, dtype=jnp.int32)
    far_ids = leaf_index[:, None] + REACH + leaf_partners[:, NEAR:]
    local_leaf = jnp.einsum(
        "ghw,gwt->ght",
        leaf_basis_transfer,
        device_middle_index[leaf_middle_owner[0]],
        precision=exact_product,
    )
    local_leaf = local_leaf + couple_rows(leaf_geom, leaf_padded[far_ids], table)
    far_product = jnp.einsum("lpk,lkr->rlp", basis, local_leaf, precision=exact_product)
    point_cloud = points.reshape(3, leaf_count, PTS)

    def near_block(block_start):
        block_leaves = block_start * 8 + jnp.arange(8, dtype=jnp.int32)
        offsets = lax.dynamic_slice_in_dim(leaf_partners[:, :NEAR], block_start * 8, 8, 0)
        partner = block_leaves[:, None] + REACH + offsets
        target_cloud = point_cloud[:, block_leaves].transpose(1, 0, 2)
        source = grid[:, partner]
        kernel = matern(target_cloud[:, None], source[RHS:].transpose(1, 2, 0, 3))
        return jnp.einsum("bjpq,rbjq->rbp", kernel, source[:RHS], precision=exact_product)

    near_blocks = lax.map(near_block, jnp.arange(leaf_count // 8, dtype=jnp.int32))
    near_product = near_blocks.transpose(1, 0, 2, 3).reshape(RHS, leaf_count, PTS)
    product = (far_product + near_product) * present[None]
    return product.reshape(RHS, leaf_count * PTS)


def solution(mesh):
    placed = (
        P(None, ("group", "leaf")),
        P(None, ("group", "leaf")),
        P(("group", "leaf")),
        P(("group", "leaf"), None, None),
        P(("group", "leaf"), None),
        P(("group", "leaf"), None),
        P(("group", "leaf"), None),
        P(("group", "leaf"), None, None),
        P(("group", "leaf"), None),
        P("group", "leaf"),
        P(("group", "leaf"), None, None),
        P(("group", "leaf"), None),
        P(("group", "leaf"), None),
        P("group", None),
        P("group", None),
    )
    return jax.shard_map(
        on_device, mesh=mesh, in_specs=placed, out_specs=P(None, ("group", "leaf")), check_vma=False
    )
```

profile of v0, /device:TPU:32, one launch (start us, length us, event | category | flops | bytes accessed | tf_op | source)
XLA Modules:
  0.0 284.0 jit_solution(18294623102038642720)
XLA Ops:
  0.0 0.8 fusion.125
  0.8 0.2 copy-done
  1.0 1.4 fusion.117
  2.4 0.1 copy.61
  2.5 0.2 reshape.349
  2.7 0.8 copy.62
  3.4 3.4 %collective-permute-start = (f32[16,516]{1,0:T(8,128)S(1)}, f32[16,516]{1,0:T(8,128)}, u32[]{:S(2)}, u32[]{:S(2)}) collective-permute-start(f32[16,516]{1,0:T(8,128)S(1)} %pad_maximum_fusion.4), channel_id=1, source_target_pairs={{0,1},{1,2},{2,3},{3,4},{4,5},{5,6},{6,7},{7,8},{8,9},{9,10},{10,1... | collective-permute-start | bytes 99080 | tf_op jit(solution)/shard_map/ppermute | solution.py:22
  6.8 4.6 %collective-permute-start.1 = (f32[16,516]{1,0:T(8,128)S(1)}, f32[16,516]{1,0:T(8,128)}, u32[]{:S(2)}, u32[]{:S(2)}) collective-permute-start(f32[16,516]{1,0:T(8,128)S(1)} %pad_maximum_fusion.4), channel_id=1, source_target_pairs={{1,0},{2,1},{3,2},{4,3},{5,4},{6,5},{7,6},{8,7},{9,8},{10,9},{11,1... | collective-permute-start | bytes 99080 | tf_op jit(solution)/shard_map/ppermute | solution.py:25
  11.4 0.7 lt.115
  12.2 0.9 broadcast_multiply_fusion
  13.1 0.8 pad_maximum_fusion.1
  13.9 1.9 collective-permute-start.2
  15.8 6.0 %collective-permute-start.3 = (f32[19,2048]{1,0:T(8,128)S(1)}, f32[19,2048]{1,0:T(8,128)S(1)}, u32[]{:S(2)}, u32[]{:S(2)}) collective-permute-start(f32[19,2048]{1,0:T(8,128)S(1)} %pad_maximum_fusion.1), channel_id=1, source_target_pairs={{1,0},{2,1},{3,2},{4,3},{5,4},{6,5},{7,6},{8,7},{9,8},{10,9},{11,1... | collective-permute-start | bytes 466952 | tf_op jit(solution)/shard_map/ppermute | solution.py:25
  21.9 1.3 convolution_bitcast_fusion.2
  23.2 0.9 fusion.119
  24.1 0.1 copy.56
  24.2 1.3 convolution_bitcast_fusion.5
  25.5 1.0 fusion.121
  26.5 0.1 copy.51
  26.7 0.2 reshape.345
  26.8 135.6 %psum.7 = f32[16,512]{1,0:T(8,128)S(1)} all-reduce(f32[16,512]{1,0:T(8,128)S(1)} %reshape.345), channel_id=1, replica_groups=mesh['group'=8,'leaf'=32] {'leaf'}, use_global_device_ids=true, to_apply=%region_0.1 | all-reduce | flops 8192 | bytes 65536 | tf_op jit(solution)/shard_map/psum | solution.py:109
  162.4 0.8 copy.52
  163.2 13.4 %all_gather.6 = f32[128,516]{1,0:T(8,128)S(1)} all-gather(f32[16,516]{1,0:T(8,128)S(1)} %pad_maximum_fusion.3), channel_id=1, replica_groups=mesh['group'=8,'leaf'=32] {'group'}, dimensions={0}, use_global_device_ids=true | all-gather | bytes 297216 | tf_op jit(solution)/shard_map/all_gather | solution.py:111
  176.8 1.1 gather_fusion.2
  178.1 0.1 reshape.347
  178.3 54.6 %all_gather.7 = f32[256,516]{1,0:T(8,128)S(1)} all-gather(f32[8,516]{1,0:T(8,128)S(1)} %pad_maximum_fusion.5), channel_id=1, replica_groups=mesh['group'=8,'leaf'=32] {'leaf'}, dimensions={0}, use_global_device_ids=true | all-gather | bytes 544896 | tf_op jit(solution)/shard_map/all_gather | solution.py:116
  233.1 0.7 gather_fusion.4
  233.9 0.2 copy.53
  234.1 0.2 copy.76
  234.3 0.2 multiply_add_fusion
  234.6 0.6 slice_bitcast_fusion.15
  235.2 2.7 reshape.346
  238.0 0.1 copy.58
  238.1 0.1 copy.77
  238.2 0.1 multiply_add_fusion.2
  238.4 0.4 reshape.348
  239.0 0.6 slice_bitcast_fusion.12
  239.6 11.0 %fusion.74 = f32[16,32,16]{1,2,0:T(8,128)S(1)} fusion(f32[16,16,32,16]{3,2,1,0:T(8,128)} %reshape.346, f32[16,16,32]{2,1,0:T(8,128)S(1)} %get-tuple-element.63, f32[16,32]{1,0:T(8,128)} %get-tuple-element.72, f32[16,16,32]{2,1,0:T(8,128)S(1)} %get-tuple-element.64, f32[16,32]{1,0:T(8,128)} %get-tuple-element.73, f32[16,16,32]{2,1,0:T(8,128)S(1)} %get-tuple-element.62, ...), kind=kOutput, calls=%fused_computation.83 | convolution fusion | flops 53477376 | bytes 661504 | tf_op jit(solution)/shard_map/njkm,njmr->nkr/dot_general | solution.py:61
  250.6 0.6 gather_fusion.3
  251.1 2.4 convolution_bitcast_fusion.3
  253.5 0.3 fusion.84
  253.9 0.6 gather_fusion.5
  254.5 0.8 pad_maximum_fusion.2
  255.3 0.8 gather_fusion.6
  256.2 0.2 copy.63
  256.4 0.2 copy.79
  256.5 0.1 multiply_add_fusion.1
  256.7 0.7 slice_bitcast_fusion.6
  257.4 0.7 reshape.350
  258.1 5.7 %fusion.81 = f32[16,32,16]{1,2,0:T(8,128)S(1)} fusion(f32[16,8,32,16]{3,2,1,0:T(8,128)S(1)} %reshape.350, f32[16,8,32]{2,1,0:T(8,128)} %get-tuple-element.66, f32[16,32]{1,0:T(8,128)S(1)} %get-tuple-element.75, f32[16,8,32]{2,1,0:T(8,128)} %get-tuple-element.67, f32[16,32]{1,0:T(8,128)} %get-tuple-element.76, f32[16,8,32]{2,1,0:T(8,128)} %get-tuple-element.65, ...), kind=kOutput, calls=%fused_computation.91 | convolution fusion | flops 26738688 | bytes 350208 | tf_op jit(solution)/shard_map/njkm,njmr->nkr/dot_general | solution.py:61
  263.8 0.5 fusion.80
  264.4 0.1 copy.82
  264.6 0.2 copy.67
  264.7 18.2 %while.10 = (s32[]{:T(128)}, f32[2,16,8,128]{3,1,2,0:T(8,128)S(1)}, s32[2]{0:T(128)S(1)}, s32[16,16]{1,0:T(8,128)S(1)}, f32[19,48,128]{2,0,1:T(8,128)S(1)}, /*in...) while((s32[]{:T(128)}, f32[2,16,8,128]{3,1,2,0:T(8,128)S(1)}, ...), condition=%wide.region_2.3_spmd, body=%wide.region_1.2_spmd.sunk | while | flops 213911856 | bytes 2398031 | solution.py:144
  265.0 0.6 dynamic_slice.11
  266.4 0.6 gather_fusion
  267.2 0.6 gather_fusion.1
  267.8 6.2 %fusion.187 = f32[2,16,8,128]{3,1,2,0:T(8,128)S(1)} fusion(f32[2,16,8,128]{3,1,2,0:T(8,128)S(1)} %get-tuple-element.144, s32[]{:T(128)} %get-tuple-element.143, f32[8,8,128]{2,1,0:T(8,128)S(1)} %bitcast.200, f32[8,128]{1,0:T(8,128)S(1)} %bitcast.208, f32[8,8,128]{2,1,0:T(8,128)S(1)} %bitcast.201, f32[8,128]{1,0:T(8,128)S(1)} %bitcast.209, ...), kind=kOutput, calls=%fused_computation.32.clone.1 | convolution fusion | flops 213909504 | bytes 700420 | tf_op jit(solution)/shard_map/while/body/eval_jaxpr/bjpq,rbjq->rbp/dot_general | solution.py:142
  273.9 0.6 dynamic_slice.11
  275.4 0.6 gather_fusion
  276.2 0.6 gather_fusion.1
  276.8 6.2 %fusion.187 = f32[2,16,8,128]{3,1,2,0:T(8,128)S(1)} fusion(f32[2,16,8,128]{3,1,2,0:T(8,128)S(1)} %get-tuple-element.144, s32[]{:T(128)} %get-tuple-element.143, f32[8,8,128]{2,1,0:T(8,128)S(1)} %bitcast.200, f32[8,128]{1,0:T(8,128)S(1)} %bitcast.208, f32[8,8,128]{2,1,0:T(8,128)S(1)} %bitcast.201, f32[8,128]{1,0:T(8,128)S(1)} %bitcast.209, ...), kind=kOutput, calls=%fused_computation.32.clone.1 | convolution fusion | flops 213909504 | bytes 700420 | tf_op jit(solution)/shard_map/while/body/eval_jaxpr/bjpq,rbjq->rbp/dot_general | solution.py:142
  282.9 0.4 fusion.79
  283.3 0.7 copy.92
  (93 shorter events, 2.0 us)
Async XLA Ops:
  0.0 1.0 copy-start
  0.0 176.6 %copy-start.9 = (s32[16,16]{1,0:T(8,128)S(1)}, s32[16,16]{1,0:T(8,128)}, u32[]{:S(2)}) copy-start(s32[16,16]{1,0:T(8,128)} %param.31) | copy-start | bytes 3076
  3.4 251.0 %collective-permute-start = (f32[16,516]{1,0:T(8,128)S(1)}, f32[16,516]{1,0:T(8,128)}, u32[]{:S(2)}, u32[]{:S(2)}) collective-permute-start(f32[16,516]{1,0:T(8,128)S(1)} %pad_maximum_fusion.4), channel_id=1, source_target_pairs={{0,1},{1,2},{2,3},{3,4},{4,5},{5,6},{6,7},{7,8},{8,9},{9,10},{10,1... | collective-permute-start | bytes 99080 | tf_op jit(solution)/shard_map/ppermute | solution.py:22
  6.8 247.6 %collective-permute-start.1 = (f32[16,516]{1,0:T(8,128)S(1)}, f32[16,516]{1,0:T(8,128)}, u32[]{:S(2)}, u32[]{:S(2)}) collective-permute-start(f32[16,516]{1,0:T(8,128)S(1)} %pad_maximum_fusion.4), channel_id=1, source_target_pairs={{1,0},{2,1},{3,2},{4,3},{5,4},{6,5},{7,6},{8,7},{9,8},{10,9},{11,1... | collective-permute-start | bytes 99080 | tf_op jit(solution)/shard_map/ppermute | solution.py:25
  13.9 250.5 %collective-permute-start.2 = (f32[19,2048]{1,0:T(8,128)S(1)}, f32[19,2048]{1,0:T(8,128)S(1)}, u32[]{:S(2)}, u32[]{:S(2)}) collective-permute-start(f32[19,2048]{1,0:T(8,128)S(1)} %pad_maximum_fusion.1), channel_id=1, source_target_pairs={{0,1},{1,2},{2,3},{3,4},{4,5},{5,6},{6,7},{7,8},{8,9},{9,10},{10,1... | collective-permute-start | bytes 466952 | tf_op jit(solution)/shard_map/ppermute | solution.py:22
  15.8 248.6 %collective-permute-start.3 = (f32[19,2048]{1,0:T(8,128)S(1)}, f32[19,2048]{1,0:T(8,128)S(1)}, u32[]{:S(2)}, u32[]{:S(2)}) collective-permute-start(f32[19,2048]{1,0:T(8,128)S(1)} %pad_maximum_fusion.1), channel_id=1, source_target_pairs={{1,0},{2,1},{3,2},{4,3},{5,4},{6,5},{7,6},{8,7},{9,8},{10,9},{11,1... | collective-permute-start | bytes 466952 | tf_op jit(solution)/shard_map/ppermute | solution.py:25
  24.1 153.9 %copy-start.6 = (f32[16,4]{0,1:T(4,128)S(1)}, f32[16,4]{0,1:T(4,128)}, u32[]{:S(2)}) copy-start(f32[16,4]{0,1:T(4,128)} %param.21) | copy-start | bytes 772
  24.1 153.9 %copy-start.7 = (f32[16,4]{0,1:T(4,128)S(1)}, f32[16,4]{0,1:T(4,128)}, u32[]{:S(2)}) copy-start(f32[16,4]{0,1:T(4,128)} %param.30) | copy-start | bytes 772
  26.6 151.5 %copy-start.12 = (s32[1,8]{1,0:T(1,128)S(1)}, s32[1,8]{1,0:T(1,128)}, u32[]{:S(2)}) copy-start(s32[1,8]{1,0:T(1,128)} %param.26) | copy-start | bytes 100
  26.7 151.6 %copy-start.8 = (f32[8,4]{0,1:T(4,128)S(1)}, f32[8,4]{0,1:T(4,128)}, u32[]{:S(2)}) copy-start(f32[8,4]{0,1:T(4,128)} %param.25) | copy-start | bytes 388
  176.6 56.4 %copy-start.10 = (s32[8,8]{1,0:T(8,128)S(1)}, s32[8,8]{1,0:T(8,128)}, u32[]{:S(2)}) copy-start(s32[8,8]{1,0:T(8,128)} %param.29) | copy-start | bytes 772
  176.6 56.4 %copy-start.11 = (s32[8,8]{1,0:T(8,128)S(1)}, s32[8,8]{1,0:T(8,128)}, u32[]{:S(2)}) copy-start(s32[8,8]{1,0:T(8,128)} %param.28) | copy-start | bytes 772
  176.8 57.1 %copy-start.13 = (s32[1,16]{1,0:T(1,128)S(1)}, s32[1,16]{1,0:T(1,128)}, u32[]{:S(2)}) copy-start(s32[1,16]{1,0:T(1,128)} %param.23) | copy-start | bytes 196
  233.8 5.0 %copy-start.5 = (s32[16,16]{1,0:T(8,128)S(1)}, s32[16,16]{1,0:T(8,128)}, u32[]{:S(2)}) copy-start(s32[16,16]{1,0:T(8,128)} %param.22) | copy-start | bytes 3076
  250.5 3.0 %copy-start.2 = (f32[8,32,32]{2,1,0:T(8,128)S(1)}, f32[8,32,32]{2,1,0:T(8,128)}, u32[]{:S(2)}) copy-start(f32[8,32,32]{2,1,0:T(8,128)} %param.27) | copy-start | bytes 98308
  258.1 5.7 %copy-start.1 = (f32[16,32,32]{2,1,0:T(8,128)S(1)}, f32[16,32,32]{2,1,0:T(8,128)}, u32[]{:S(2)}) copy-start(f32[16,32,32]{2,1,0:T(8,128)} %param.24) | copy-start | bytes 196612
  258.1 6.2 %copy-start.3 = (f32[3,2048]{1,0:T(4,128)S(1)}, f32[3,2048]{1,0:T(4,128)}, u32[]{:S(2)}) copy-start(f32[3,2048]{1,0:T(4,128)} %param.17) | copy-start | bytes 73732
  263.8 1.0 copy-start.4
where the time goes:
time: 285 us; the launch traced here: 284 us
  blocking collectives  204 us (72%)
  matrix products  38.4 us (13%)
  local copies, waits for them, and re-layouts  19.3 us (7%)
  starting transfers between devices  15.9 us (6%)
  other arithmetic  4.5 us (2%)
    psum x1, blocking collectives, on_device(): coeff_top = lax.psum(partial_top, 'leaf')  136 us
    all_gather x1, blocking collectives, on_device(): mid_all = lax.all_gather(mid_rows, 'leaf', axis=0, tiled=True)  54.6 us
    dot_general x3, matrix products, couple_rows(): jnp.einsum('njkm,njmr->nkr', coupling, source_coeff, precision=exact_prod...  19 us
    all_gather x1, blocking collectives, on_device(): top_all = lax.all_gather(top_rows, 'group', axis=0, tiled=True)  13.4 us
    dot_general x2, matrix products, near_block(): jnp.einsum('bjpq,rbjq->rbp', kernel, source[:RHS], precision=exact_product)  12.4 us
    ppermute x2, starting transfers between devices, extended(): lax.ppermute(lax.slice_in_dim(block, 0, width, axis=dim), axis, backward)  10.6 us
  transfers between devices with their start and end apart: 4, of which 0 were waited for; matrix products, arithmetic and copies ran while one was open for 14% of the time, Pallas kernels for 0%

commit v1 on v0

--- a/solution.py
+++ b/solution.py
@@ -106,7 +106,7 @@
     )
     raised = jnp.einsum("mkj,mkr->mjr", mid_transfer, coeff_mid, precision=exact_product)
     partial_top = jnp.einsum("tm,mjr->tjr", top_members, raised, precision=exact_product)
-    coeff_top = lax.psum(partial_top, "leaf")
+    coeff_top = jnp.sum(lax.all_gather(partial_top, "leaf"), 0)
     top_rows = jnp.concatenate([coeff_top.reshape(TOP, coeff_width), top_geom], axis=1)
     top_all = lax.all_gather(top_rows, "group", axis=0, tiled=True)
     total_tops = top_all.shape[0]

time: 285 us -> 166 us (0.58)
  blocking collectives: 204 us -> 66.6 us
  between operations: 0.6 us -> 13.9 us
  other arithmetic: 4.5 us -> 8.08 us
    psum x1 -> x0, blocking collectives: 136 us -> none  [on_device(): coeff_top = lax.psum(partial_top, 'leaf')]
  transfers between devices with their start and end apart: 4 -> 5, of which waited for: 0 -> 0; matrix products, arithmetic and copies ran while one was open for 14% -> 25% of each run, Pallas kernels for 0% -> 0%
where the time goes in v1:
time: 166 us; the launch traced here: 165 us
  blocking collectives  66.6 us (40%)
  matrix products  39.5 us (24%)
  local copies, waits for them, and re-layouts  19.3 us (12%)
  starting transfers between devices  15.9 us (10%)
  between operations  13.9 us (8%)
  other arithmetic  8.08 us (5%)
    all_gather x1, blocking collectives, on_device(): mid_all = lax.all_gather(mid_rows, 'leaf', axis=0, tiled=True)  53 us
    dot_general x3, matrix products, couple_rows(): jnp.einsum('njkm,njmr->nkr', coupling, source_coeff, precision=exact_prod...  19.5 us
    all_gather x1, blocking collectives, on_device(): top_all = lax.all_gather(top_rows, 'group', axis=0, tiled=True)  13.5 us
    dot_general x2, matrix products, near_block(): jnp.einsum('bjpq,rbjq->rbp', kernel, source[:RHS], precision=exact_product)  12.4 us
    ppermute x2, starting transfers between devices, extended(): lax.ppermute(lax.slice_in_dim(block, 0, width, axis=dim), axis, backward)  10.6 us
    ppermute x2, starting transfers between devices, extended(): lax.ppermute(lax.slice_in_dim(block, block.shape[dim] - width, None, axis...  5.31 us
    reshape x3, local copies, waits for them, and re-layouts, couple_rows(): source_point_rows[..., :coeff_width]  4.05 us
  transfers between devices with their start and end apart: 5, of which 0 were waited for; matrix products, arithmetic and copies ran while one was open for 25% of the time, Pallas kernels for 0%

profile of v1, /device:TPU:32, one launch (start us, length us, event | category | flops | bytes accessed | tf_op | source)
XLA Modules:
  0.0 165.0 jit_solution(4693450394896980222)
XLA Ops:
  6.6 0.8 fusion.125
  7.5 0.1 copy-done
  7.6 1.4 fusion.117
  9.0 0.1 copy.81
  9.1 0.2 reshape.349
  9.3 0.8 copy.82
  10.1 3.4 %collective-permute-start = (f32[16,516]{1,0:T(8,128)S(1)}, f32[16,516]{1,0:T(8,128)S(1)}, u32[]{:S(2)}, u32[]{:S(2)}) collective-permute-start(f32[16,516]{1,0:T(8,128)S(1)} %pad_maximum_fusion.4), channel_id=1, source_target_pairs={{0,1},{1,2},{2,3},{3,4},{4,5},{5,6},{6,7},{7,8},{8,9},{9,10},{10,1... | collective-permute-start | bytes 99080 | tf_op jit(solution)/shard_map/ppermute | solution.py:22
  13.5 4.6 %collective-permute-start.1 = (f32[16,516]{1,0:T(8,128)S(1)}, f32[16,516]{1,0:T(8,128)S(1)}, u32[]{:S(2)}, u32[]{:S(2)}) collective-permute-start(f32[16,516]{1,0:T(8,128)S(1)} %pad_maximum_fusion.4), channel_id=1, source_target_pairs={{1,0},{2,1},{3,2},{4,3},{5,4},{6,5},{7,6},{8,7},{9,8},{10,9},{11,1... | collective-permute-start | bytes 99080 | tf_op jit(solution)/shard_map/ppermute | solution.py:25
  18.0 0.7 lt.115
  18.8 0.9 broadcast_multiply_fusion
  19.7 0.8 pad_maximum_fusion.1
  20.5 1.9 %collective-permute-start.2 = (f32[19,2048]{1,0:T(8,128)S(1)}, f32[19,2048]{1,0:T(8,128)S(1)}, u32[]{:S(2)}, u32[]{:S(2)}) collective-permute-start(f32[19,2048]{1,0:T(8,128)S(1)} %pad_maximum_fusion.1), channel_id=1, source_target_pairs={{0,1},{1,2},{2,3},{3,4},{4,5},{5,6},{6,7},{7,8},{8,9},{9,10},{10,1... | collective-permute-start | bytes 466952 | tf_op jit(solution)/shard_map/ppermute | solution.py:22
  22.4 6.0 %collective-permute-start.3 = (f32[19,2048]{1,0:T(8,128)S(1)}, f32[19,2048]{1,0:T(8,128)S(1)}, u32[]{:S(2)}, u32[]{:S(2)}) collective-permute-start(f32[19,2048]{1,0:T(8,128)S(1)} %pad_maximum_fusion.1), channel_id=1, source_target_pairs={{1,0},{2,1},{3,2},{4,3},{5,4},{6,5},{7,6},{8,7},{9,8},{10,9},{11,1... | collective-permute-start | bytes 466952 | tf_op jit(solution)/shard_map/ppermute | solution.py:25
  28.4 1.3 convolution_bitcast_fusion.2
  29.7 0.9 fusion.119
  30.7 1.3 convolution_bitcast_fusion.5
  32.0 1.6 fusion.121
  33.8 0.7 slice_bitcast_fusion.19
  34.5 0.7 fusion.148
  35.1 0.1 reshape.347
  35.2 0.8 copy.77
  36.0 53.0 %all_gather.15 = f32[256,516]{1,0:T(8,128)S(1)} all-gather(f32[8,516]{1,0:T(8,128)S(1)} %pad_maximum_fusion.5), channel_id=1, replica_groups=mesh['group'=8,'leaf'=32] {'leaf'}, dimensions={0}, use_global_device_ids=true | all-gather | bytes 544896 | tf_op jit(solution)/shard_map/all_gather | solution.py:116
  89.1 0.7 gather_fusion.4
  90.3 0.6 pad_clamp_fusion.5
  90.9 0.1 copy.78
  91.0 0.1 copy.97
  91.1 0.1 multiply_add_fusion.2
  91.3 0.4 reshape.348
  91.7 0.6 pad_clamp_fusion.3
  92.5 3.0 %convolution_bitcast_fusion.3 = f32[8,32,16]{1,2,0:T(8,128)} fusion(f32[8,8,32,16]{3,2,1,0:T(8,128)S(1)} %reshape.348, f32[8,8,32]{2,1,0:T(8,128)S(1)} %get-tuple-element.75, f32[8,32]{1,0:T(8,128)S(1)} %get-tuple-element.84, f32[8,8,32]{2,1,0:T(8,128)S(1)} %get-tuple-element.76, f32[8,32]{1,0:T(8,128)S(1)} %get-tuple-element.85, ...), kind=kOutput, calls=%fused_computation.92 | convolution fusion | flops 13369344 | bytes 175104 | tf_op jit(solution)/shard_map/njkm,njmr->nkr/dot_general | solution.py:61
  95.6 0.8 gather_fusion.6
  96.6 0.2 copy.83
  96.7 0.2 copy.99
  96.9 0.1 multiply_add_fusion.1
  97.1 0.7 slice_bitcast_fusion.6
  97.8 0.7 reshape.350
  98.5 5.6 %fusion.81 = f32[16,32,16]{1,2,0:T(8,128)S(1)} fusion(f32[16,8,32,16]{3,2,1,0:T(8,128)S(1)} %reshape.350, f32[16,8,32]{2,1,0:T(8,128)} %get-tuple-element.72, f32[16,32]{1,0:T(8,128)S(1)} %get-tuple-element.81, f32[16,8,32]{2,1,0:T(8,128)} %get-tuple-element.73, f32[16,32]{1,0:T(8,128)S(1)} %get-tuple-element.82, f32[16,8,32]{2,1,0:T(8,128)} %get-tuple-element.71, ...), kind=kOutput, calls=%fused_computation.91 | convolution fusion | flops 26738688 | bytes 350208 | tf_op jit(solution)/shard_map/njkm,njmr->nkr/dot_general | solution.py:61
  104.2 0.1 copy.102
  104.3 0.2 copy.87
  104.5 18.3 %while.10 = (s32[]{:T(128)}, f32[2,16,8,128]{3,1,2,0:T(8,128)S(1)}, s32[2]{0:T(128)S(1)}, s32[16,16]{1,0:T(8,128)S(1)}, f32[19,48,128]{2,0,1:T(8,128)S(1)}, /*in...) while((s32[]{:T(128)}, f32[2,16,8,128]{3,1,2,0:T(8,128)S(1)}, ...), condition=%wide.region_2.3_spmd, body=%wide.region_1.2_spmd.sunk | while | flops 213911856 | bytes 2398031 | solution.py:144
  104.7 0.7 dynamic_slice.11
  106.2 0.6 gather_fusion
  107.0 0.6 gather_fusion.1
  107.5 6.2 %fusion.187 = f32[2,16,8,128]{3,1,2,0:T(8,128)S(1)} fusion(f32[2,16,8,128]{3,1,2,0:T(8,128)S(1)} %get-tuple-element.150, s32[]{:T(128)} %get-tuple-element.149, f32[8,8,128]{2,1,0:T(8,128)S(1)} %bitcast.202, f32[8,128]{1,0:T(8,128)S(1)} %bitcast.210, f32[8,8,128]{2,1,0:T(8,128)S(1)} %bitcast.203, f32[8,128]{1,0:T(8,128)S(1)} %bitcast.211, ...), kind=kOutput, calls=%fused_computation.32.clone.1 | convolution fusion | flops 213909504 | bytes 700420 | tf_op jit(solution)/shard_map/while/body/eval_jaxpr/bjpq,rbjq->rbp/dot_general | solution.py:142
  113.7 0.7 dynamic_slice.11
  115.2 0.6 gather_fusion
  116.0 0.6 gather_fusion.1
  116.6 6.2 %fusion.187 = f32[2,16,8,128]{3,1,2,0:T(8,128)S(1)} fusion(f32[2,16,8,128]{3,1,2,0:T(8,128)S(1)} %get-tuple-element.150, s32[]{:T(128)} %get-tuple-element.149, f32[8,8,128]{2,1,0:T(8,128)S(1)} %bitcast.202, f32[8,128]{1,0:T(8,128)S(1)} %bitcast.210, f32[8,8,128]{2,1,0:T(8,128)S(1)} %bitcast.203, f32[8,128]{1,0:T(8,128)S(1)} %bitcast.211, ...), kind=kOutput, calls=%fused_computation.32.clone.1 | convolution fusion | flops 213909504 | bytes 700420 | tf_op jit(solution)/shard_map/while/body/eval_jaxpr/bjpq,rbjq->rbp/dot_general | solution.py:142
  122.8 2.5 %reduce_sum.9 = f32[16,32,16]{1,0,2:T(8,128)S(1)} reduce(f32[32,16,32,16]{2,1,0,3:T(8,128)} %bitcast.190, f32[]{:T(128)} %constant.59.clone.1), dimensions={0}, to_apply=%region_0.1 | reduce | flops 253952 | bytes 1081348 | tf_op jit(solution)/shard_map/reduce_sum | solution.py:109
  125.3 0.1 copy.71
  125.4 0.2 reshape.345
  125.6 13.5 %all_gather.14 = f32[128,516]{1,0:T(8,128)S(1)} all-gather(f32[16,516]{1,0:T(8,128)S(1)} %pad_maximum_fusion.3), channel_id=1, replica_groups=mesh['group'=8,'leaf'=32] {'group'}, dimensions={0}, use_global_device_ids=true | all-gather | bytes 297216 | tf_op jit(solution)/shard_map/all_gather | solution.py:111
  139.1 1.1 gather_fusion.2
  140.4 0.2 copy.73
  140.5 0.2 copy.96
  140.7 0.2 multiply_add_fusion
  141.0 3.0 %reshape.346 = f32[16,16,32,16]{3,2,1,0:T(8,128)} reshape(f32[16,16,512]{2,1,0:T(8,128)S(1)} %slice.202) | data formatting | bytes 1048576 | tf_op jit(solution)/shard_map/reshape | solution.py:57
  144.0 10.9 %fusion.74 = f32[16,32,16]{1,2,0:T(8,128)S(1)} fusion(f32[16,16,32,16]{3,2,1,0:T(8,128)} %reshape.346, f32[16,16,32]{2,1,0:T(8,128)S(1)} %get-tuple-element.69, f32[16,32]{1,0:T(8,128)S(1)} %get-tuple-element.78, f32[16,16,32]{2,1,0:T(8,128)S(1)} %get-tuple-element.70, f32[16,32]{1,0:T(8,128)S(1)} %get-tuple-element.79, ...), kind=kOutput, calls=%fused_computation.83 | convolution fusion | flops 53477376 | bytes 661504 | tf_op jit(solution)/shard_map/njkm,njmr->nkr/dot_general | solution.py:61
  154.8 0.7 gather_fusion.3
  155.6 0.3 fusion.84
  155.9 0.7 gather_fusion.5
  156.6 0.5 fusion.80
  157.1 0.4 fusion.79
  157.5 0.7 copy.112
  (94 shorter events, 2.1 us)
Async XLA Ops:
  6.5 1.0 copy-start
  6.5 83.7 %copy-start.6 = (f32[16,4]{0,1:T(4,128)S(1)}, f32[16,4]{0,1:T(4,128)}, u32[]{:S(2)}) copy-start(f32[16,4]{0,1:T(4,128)} %param.21) | copy-start | bytes 772
  6.5 83.4 %copy-start.12 = (s32[1,16]{1,0:T(1,128)S(1)}, s32[1,16]{1,0:T(1,128)}, u32[]{:S(2)}) copy-start(s32[1,16]{1,0:T(1,128)} %param.23) | copy-start | bytes 196
  6.5 83.4 %copy-start.8 = (f32[8,4]{0,1:T(4,128)S(1)}, f32[8,4]{0,1:T(4,128)}, u32[]{:S(2)}) copy-start(f32[8,4]{0,1:T(4,128)} %param.25) | copy-start | bytes 388
  6.5 82.5 %copy-start.11 = (s32[8,8]{1,0:T(8,128)S(1)}, s32[8,8]{1,0:T(8,128)}, u32[]{:S(2)}) copy-start(s32[8,8]{1,0:T(8,128)} %param.28) | copy-start | bytes 772
  6.5 82.5 %copy-start.10 = (s32[8,8]{1,0:T(8,128)S(1)}, s32[8,8]{1,0:T(8,128)}, u32[]{:S(2)}) copy-start(s32[8,8]{1,0:T(8,128)} %param.29) | copy-start | bytes 772
  6.6 83.4 %copy-start.9 = (s32[16,16]{1,0:T(8,128)S(1)}, s32[16,16]{1,0:T(8,128)}, u32[]{:S(2)}) copy-start(s32[16,16]{1,0:T(8,128)} %param.31) | copy-start | bytes 3076
  6.6 83.6 %copy-start.7 = (f32[16,4]{0,1:T(4,128)S(1)}, f32[16,4]{0,1:T(4,128)}, u32[]{:S(2)}) copy-start(f32[16,4]{0,1:T(4,128)} %param.30) | copy-start | bytes 772
  6.6 85.7 %copy-start.4 = (s32[16,16]{1,0:T(8,128)S(1)}, s32[16,16]{1,0:T(8,128)}, u32[]{:S(2)}) copy-start(s32[16,16]{1,0:T(8,128)} %param.22) | copy-start | bytes 3076
  6.6 116.2 %all-gather.3.cloned.1.call-start = ((), (), s32[]{:S(2)}) async-start(), calls=%async_computation | async-start | bytes 4325376 | tf_op jit(solution)/shard_map/all_gather | solution.py:109
  10.1 85.5 %collective-permute-start = (f32[16,516]{1,0:T(8,128)S(1)}, f32[16,516]{1,0:T(8,128)S(1)}, u32[]{:S(2)}, u32[]{:S(2)}) collective-permute-start(f32[16,516]{1,0:T(8,128)S(1)} %pad_maximum_fusion.4), channel_id=1, source_target_pairs={{0,1},{1,2},{2,3},{3,4},{4,5},{5,6},{6,7},{7,8},{8,9},{9,10},{10,1... | collective-permute-start | bytes 99080 | tf_op jit(solution)/shard_map/ppermute | solution.py:22
  13.5 82.2 %collective-permute-start.1 = (f32[16,516]{1,0:T(8,128)S(1)}, f32[16,516]{1,0:T(8,128)S(1)}, u32[]{:S(2)}, u32[]{:S(2)}) collective-permute-start(f32[16,516]{1,0:T(8,128)S(1)} %pad_maximum_fusion.4), channel_id=1, source_target_pairs={{1,0},{2,1},{3,2},{4,3},{5,4},{6,5},{7,6},{8,7},{9,8},{10,9},{11,1... | collective-permute-start | bytes 99080 | tf_op jit(solution)/shard_map/ppermute | solution.py:25
  20.5 83.6 %collective-permute-start.2 = (f32[19,2048]{1,0:T(8,128)S(1)}, f32[19,2048]{1,0:T(8,128)S(1)}, u32[]{:S(2)}, u32[]{:S(2)}) collective-permute-start(f32[19,2048]{1,0:T(8,128)S(1)} %pad_maximum_fusion.1), channel_id=1, source_target_pairs={{0,1},{1,2},{2,3},{3,4},{4,5},{5,6},{6,7},{7,8},{8,9},{9,10},{10,1... | collective-permute-start | bytes 466952 | tf_op jit(solution)/shard_map/ppermute | solution.py:22
  22.4 81.7 %collective-permute-start.3 = (f32[19,2048]{1,0:T(8,128)S(1)}, f32[19,2048]{1,0:T(8,128)S(1)}, u32[]{:S(2)}, u32[]{:S(2)}) collective-permute-start(f32[19,2048]{1,0:T(8,128)S(1)} %pad_maximum_fusion.1), channel_id=1, source_target_pairs={{1,0},{2,1},{3,2},{4,3},{5,4},{6,5},{7,6},{8,7},{9,8},{10,9},{11,1... | collective-permute-start | bytes 466952 | tf_op jit(solution)/shard_map/ppermute | solution.py:25
  98.5 5.7 %copy-start.3 = (f32[3,2048]{1,0:T(4,128)S(1)}, f32[3,2048]{1,0:T(4,128)}, u32[]{:S(2)}) copy-start(f32[3,2048]{1,0:T(4,128)} %param.17) | copy-start | bytes 73732
  144.0 11.6 %copy-start.2 = (f32[8,32,32]{2,1,0:T(8,128)S(1)}, f32[8,32,32]{2,1,0:T(8,128)}, u32[]{:S(2)}) copy-start(f32[8,32,32]{2,1,0:T(8,128)} %param.27) | copy-start | bytes 98308
  144.0 11.6 %copy-start.5 = (f32[8,32,16]{1,2,0:T(8,128)S(1)}, f32[8,32,16]{1,2,0:T(8,128)}, u32[]{:S(2)}) copy-start(f32[8,32,16]{1,2,0:T(8,128)} %convolution_bitcast_fusion.3) | copy-start | bytes 49156
  144.0 12.6 %copy-start.1 = (f32[16,32,32]{2,1,0:T(8,128)S(1)}, f32[16,32,32]{2,1,0:T(8,128)}, u32[]{:S(2)}) copy-start(f32[16,32,32]{2,1,0:T(8,128)} %param.24) | copy-start | bytes 196612
Sparse Core Ops, SparseCore 0:
  33.8 87.0 all-gather.2
